TPU v7x, 32 devices: a whole 2x2x4 slice. The times are simulated.
32 devices in a mesh: row: 8 (over z, x), col: 4 (over y, core).
Axes of the slice: x: 2, y: 2, z: 4, core: 2. Of those that a mesh axis runs over, the one named last changes fastest.
Arguments:
- solution_field: float32 [32, 32768], P(None, ('row', 'col')), may hold values from -6 to 6
- residual: float32 [32, 32768], P(None, ('row', 'col')), may hold values from -420 to 420
- direction: float32 [32, 32768], P(None, ('row', 'col')), may hold values from -420 to 420
- positions: bfloat16 [2, 32768], P(None, ('row', 'col')), may hold values from -6 to 6
- tile_pairs: int32 [2, 49152], P(None, ('row', 'col')), may hold values from 0 to 63, as said below
- pair_count: int32 [32], P(('row', 'col')), may hold values from 0 to 1536, as said below
Outputs:
- solution_next: float32 [32, 32768], P(None, ('row', 'col'))
- residual_next: float32 [32, 32768], P(None, ('row', 'col'))
- direction_next: float32 [32, 32768], P(None, ('row', 'col'))
Inputs may be any that keep to these rules, and one draw needn't show every extreme that they name: `tile_pairs`: row 0 holds local row tiles below 32, row 1 local column tiles below 64. The live pairs of one slot block are distinct and strictly upper (I < J); entries in slots that are not live are in range but carry nothing. `pair_count`: some slot block is full in every draw.
All inputs are finite; a program needn't handle non-finite values.
Results may differ from a plain program's by a relative error of at most 0.007.
Values may be sent and summed in bfloat16 or wider, within the bound.
A program may use at most 64 MiB of HBM per device.

v0:
```python
import math

import jax
import jax.numpy as jnp
from jax import lax
from jax.sharding import PartitionSpec as P

TILE = 128


AMPLITUDE = 0.025
NUGGET = 2.0
RADIUS = 1.0
HIGHEST = lax.Precision.HIGHEST


def kernel_tile(near_side, far_side):
    differ = near_side[..., :, None] - far_side[..., None, :]
    distance = jnp.sqrt(jnp.sum(differ * differ, axis=0)) / RADIUS
    remain = jnp.maximum(1.0 - distance, 0.0)
    return AMPLITUDE * remain**4 * (4.0 * distance + 1.0)


def cross_gram_matrix(former, latter):
    return lax.dot_general(
        former,
        latter,
        (((1,), (1,)), ((), ())),
        precision=HIGHEST,
        preferred_element_type=jnp.float32,
    )


def apply_left(matrix, vectors):
    return jnp.dot(matrix.T, vectors, precision=HIGHEST)


def symmetric_solve(matrix, target):
    balanced = 0.5 * (matrix + matrix.T)
    factor = jnp.linalg.cholesky(balanced)
    middle = lax.linalg.triangular_solve(factor, target, left_side=True, lower=True)
    return lax.linalg.triangular_solve(factor, middle, left_side=True, lower=True, transpose_a=True)


def on_device(solution_field, residual, direction, positions, tile_pairs, pair_count):
    probes, own_points = direction.shape
    own_tiles = own_points // TILE
    dir_half = direction.astype(jnp.bfloat16)
    row_dir, row_pos = (
        lax.all_gather(dir_half, "col", axis=1, tiled=True),
        lax.all_gather(positions, "col", axis=1, tiled=True),
    )
    col_dir, col_pos = (
        lax.all_gather(dir_half, "row", axis=1, tiled=True),
        lax.all_gather(positions, "row", axis=1, tiled=True),
    )
    own_pos = positions.astype(jnp.float32).reshape(2, own_tiles, TILE)
    diagonal = kernel_tile(own_pos, own_pos).astype(jnp.bfloat16)
    own_product = jnp.einsum(
        "npq,knq->knp",
        diagonal,
        dir_half.reshape(probes, own_tiles, TILE),
        preferred_element_type=jnp.float32,
    ).reshape(probes, own_points)
    row_tiles = row_dir.shape[1] // TILE
    col_tiles = col_dir.shape[1] // TILE
    row_vector = row_dir.reshape(probes, row_tiles, TILE)
    column_vector = col_dir.reshape(probes, col_tiles, TILE)
    row_coord = row_pos.reshape(2, row_tiles, TILE)
    col_coord = col_pos.reshape(2, col_tiles, TILE)
    row_range = jnp.arange(row_tiles, dtype=jnp.int32)
    col_range = jnp.arange(col_tiles, dtype=jnp.int32)
    slot_total = tile_pairs.shape[1]
    block_size = math.gcd(slot_total, 64)
    live_count = pair_count[0]

    def stepped(block_no, running_totals):
        row_acc, col_acc = running_totals
        first_slot = block_no * block_size
        row_index = lax.dynamic_slice_in_dim(tile_pairs[0], first_slot, block_size)
        col_index = lax.dynamic_slice_in_dim(tile_pairs[1], first_slot, block_size)
        live_mask = first_slot + jnp.arange(block_size, dtype=jnp.int32) < live_count
        row_chosen_index = (row_index[:, None] == row_range[None, :]).astype(jnp.bfloat16)
        column_chosen_index = (col_index[:, None] == col_range[None, :]).astype(jnp.bfloat16)
        near_side = jnp.einsum(
            "bt,ctq->cbq", row_chosen_index, row_coord, preferred_element_type=jnp.float32
        )
        far_side = jnp.einsum(
            "bt,ctq->cbq", column_chosen_index, col_coord, preferred_element_type=jnp.float32
        )
        row_sel = jnp.einsum(
            "di,siz->sdz", row_chosen_index, row_vector, preferred_element_type=jnp.float32
        ).astype(jnp.bfloat16)
        col_sel = jnp.einsum(
            "di,siz->sdz", column_chosen_index, column_vector, preferred_element_type=jnp.float32
        ).astype(jnp.bfloat16)
        kernel_block = kernel_tile(near_side, far_side)
        kernel_block = jnp.where(live_mask[:, None, None], kernel_block, 0.0).astype(jnp.bfloat16)
        forward_step = jnp.einsum(
            "bpq,kbq->kbp", kernel_block, col_sel, preferred_element_type=jnp.float32
        )
        backward = jnp.einsum(
            "bpq,kbp->kbq", kernel_block, row_sel, preferred_element_type=jnp.float32
        )
        row_add = jnp.einsum(
            "bt,kbp->ktp",
            row_chosen_index.astype(jnp.float32),
            forward_step,
            precision=HIGHEST,
            preferred_element_type=jnp.float32,
        )
        col_add = jnp.einsum(
            "au,lax->lux",
            column_chosen_index.astype(jnp.float32),
            backward,
            precision=HIGHEST,
            preferred_element_type=jnp.float32,
        )
        return (row_acc + row_add, col_acc + col_add)

    start_totals = (
        jnp.zeros((probes, row_tiles, TILE), jnp.float32),
        jnp.zeros((probes, col_tiles, TILE), jnp.float32),
    )
    row_acc, col_acc = lax.fori_loop(0, slot_total // block_size, stepped, start_totals)
    row_flat = row_acc.reshape(probes, row_tiles * TILE)
    col_flat = col_acc.reshape(probes, col_tiles * TILE)
    row_whole = lax.psum(row_flat.astype(jnp.bfloat16), "col").astype(jnp.float32)
    row_part = lax.dynamic_slice_in_dim(
        row_whole, lax.axis_index("col") * own_points, own_points, 1
    )
    col_whole = lax.psum(col_flat.astype(jnp.bfloat16), "row").astype(jnp.float32)
    col_part = lax.dynamic_slice_in_dim(
        col_whole, lax.axis_index("row") * own_points, own_points, 1
    )
    applied = NUGGET * direction + own_product + row_part + col_part
    curvature, crossing, norm_old, image_resid, square = lax.psum(
        (
            cross_gram_matrix(direction, applied),
            cross_gram_matrix(direction, residual),
            cross_gram_matrix(residual, residual),
            cross_gram_matrix(applied, residual),
            cross_gram_matrix(applied, applied),
        ),
        ("row", "col"),
    )
    step_size = symmetric_solve(curvature, crossing)
    residual_next = residual - apply_left(step_size, applied)
    shifted = jnp.dot(step_size.T, image_resid, precision=HIGHEST)
    quadratic = jnp.dot(
        step_size.T, jnp.dot(square, step_size, precision=HIGHEST), precision=HIGHEST
    )
    norm_new = norm_old - shifted - shifted.T + quadratic
    solution_next = solution_field + apply_left(step_size, direction)
    mix_weight = symmetric_solve(norm_old, norm_new)
    direction_next = residual_next + apply_left(mix_weight, direction)
    return (solution_next, residual_next, direction_next)


def solution(mesh):
    in_specs = (
        P(None, ("row", "col")),
        P(None, ("row", "col")),
        P(None, ("row", "col")),
        P(None, ("row", "col")),
        P(None, ("row", "col")),
        P(("row", "col")),
    )
    out_specs = (P(None, ("row", "col")), P(None, ("row", "col")), P(None, ("row", "col")))
    return jax.shard_map(
        on_device, mesh=mesh, in_specs=in_specs, out_specs=out_specs, check_vma=False
    )
```

profile of v0, /device:TPU:0, one launch (start us, length us, event | category | flops | bytes accessed | tf_op | source)
XLA Modules:
  0.0 675.7 jit_solution(7881946723567846366)
XLA Ops:
  8.1 33.0 %all_gather.12 = bf16[32,8192]{1,0:T(8,128)(2,1)S(1)} all-gather(bf16[32,1024]{1,0:T(8,128)(2,1)S(1)} %convert_element_type.65), channel_id=1, replica_groups=mesh['row'=8,'col'=4] {'row'}, dimensions={1}, use_global_device_ids=true | all-gather | bytes 589824 | tf_op jit(solution)/shard_map/all_gather | solution.py:54
  41.2 5.8 all_gather.15
  46.9 30.7 %all_gather.14 = bf16[2,8192]{1,0:T(2,128)(2,1)S(1)} all-gather(bf16[2,1024]{1,0:T(2,128)(2,1)} %param.16), channel_id=1, replica_groups=mesh['row'=8,'col'=4] {'row'}, dimensions={1}, use_global_device_ids=true | all-gather | bytes 36864 | tf_op jit(solution)/shard_map/all_gather | solution.py:55
  77.7 5.3 all_gather.13
  84.0 413.3 %while.16 = (s32[]{:T(128)}, f32[32,32,128]{2,1,0:T(8,128)}, f32[32,64,128]{2,1,0:T(8,128)}, s32[2,1536]{1,0:T(2,128)}, bf16[32,64,128]{2,1,0:T(8,128)(2,1)}, /*...) while((s32[]{:T(128)}, f32[32,32,128]{2,1,0:T(8,128)}, ...), condition=%wide.region_3.4_spmd.clone, body=%wide.region_1.3_spmd.clone.sunk | while | flops 506742912 | bytes 25242432 | solution.py:125
  107.3 3.5 fusion.128
  124.6 3.5 fusion.128
  141.9 3.5 fusion.128
  159.2 3.5 fusion.128
  176.5 3.5 fusion.128
  193.9 3.5 fusion.128
  211.2 3.5 fusion.128
  228.5 3.5 fusion.128
  245.8 3.5 fusion.128
  263.1 3.5 fusion.128
  280.4 3.5 fusion.128
  297.7 3.5 fusion.128
  315.1 3.5 fusion.128
  332.4 3.5 fusion.128
  384.3 3.5 fusion.128
  470.9 3.5 fusion.128
  503.2 29.6 %all-reduce.4.cloned.1.call-done = bf16[32,4096]{1,0:T(8,128)(2,1)} async-done(((bf16[32,4096]{1,0:T(8,128)(2,1)}), bf16[32,4096]{1,0:T(8,128)(2,1)}) %all-reduce.4.cloned.1.call-update) | async-done | bytes 262160 | tf_op jit(solution)/shard_map/psum | solution.py:128
  532.8 76.2 %all-reduce.6.cloned.1.call-done = bf16[32,8192]{1,0:T(8,128)(2,1)} async-done(((bf16[32,8192]{1,0:T(8,128)(2,1)}), bf16[32,8192]{1,0:T(8,128)(2,1)}) %all-reduce.6.cloned.1.call-update) | async-done | bytes 524304 | tf_op jit(solution)/shard_map/psum | solution.py:132
  610.7 40.8 %all-reduce = (f32[32,32]{1,0:T(8,128)S(1)}, f32[32,32]{1,0:T(8,128)S(1)}, f32[32,32]{1,0:T(8,128)S(1)}, f32[32,32]{1,0:T(8,128)S(1)}, f32[32,32]{1,0:T(8,128)S(1)}) all-reduce(f32[32,32]{1,0:T(8,128)S(1)} %fusion.49, f32[32,32]{1,0:T(8,128)S(1)} %convolution_bitcast_fusion.7, ...), channel_id=1, replica_groups=mesh['row'=8,'col'=4] {'row','col'}, use_global_device_ids=true, to_apply=%region_9.0 | all-reduce | flops 5120 | bytes 40960 | tf_op jit(solution)/shard_map/psum | solution.py:137
  (359 shorter events, 382.1 us)
Async XLA Ops:
  7.2 525.6 %all-reduce.4.cloned.1.call-start = ((), (), s32[]{:S(2)}) async-start(), calls=%async_computation | async-start | bytes 524288 | tf_op jit(solution)/shard_map/psum | solution.py:128
  497.3 4.6 copy-start.4
  497.3 4.9 copy-start
  497.3 5.3 copy-start.1
  499.3 167.7 %copy-start.3 = (f32[32,1024]{1,0:T(8,128)S(1)}, f32[32,1024]{1,0:T(8,128)}, u32[]{:S(2)}) copy-start(f32[32,1024]{1,0:T(8,128)} %param.13) | copy-start | bytes 393220
  499.3 109.7 %all-reduce.6.cloned.1.call-start = ((), (), s32[]{:S(2)}) async-start(), calls=%async_computation.1 | async-start | bytes 1048576 | tf_op jit(solution)/shard_map/psum | solution.py:132
  665.9 3.0 copy-start.2
Sparse Core Ops, SparseCore 0:
  499.4 33.3 all-reduce.3
  536.2 72.7 all-reduce.5
where the time goes:
time: 681 us; the launch traced here: 676 us
  matrix products  255 us (37%)
  other arithmetic  159 us (23%)
  blocking collectives  116 us (17%)
  waiting for transfers between devices  106 us (16%)
  local copies, waits for them, and re-layouts  24.3 us (4%)
  between operations  14.3 us (2%)
    dot_general x24, matrix products, stepped(): jnp.einsum('au,lax->lux', column_chosen_index.astype(jnp.float32), backwa...  83.6 us
    psum x1, waiting for transfers between devices, on_device(): lax.psum(col_flat.astype(jnp.bfloat16), 'row').astype(jnp.float32)  76.2 us
    dot_general x24, matrix products, stepped(): jnp.einsum('bt,kbp->ktp', row_chosen_index.astype(jnp.float32), forward_s...  70.3 us
    reduce_sum x25, other arithmetic, kernel_tile(): distance = jnp.sqrt(jnp.sum(differ * differ, axis=0)) / RADIUS  66.6 us
    convert_element_type x24, other arithmetic, stepped(): jnp.where(live_mask[:, None, None], kernel_block, 0.0).astype(jnp.bfloat16)  59 us
    psum x1, blocking collectives, on_device(): lax.psum((cross_gram_matrix(direction, applied), cross_gram_matrix(direct...  40.8 us
    dot_general x24, matrix products, stepped(): jnp.einsum('di,siz->sdz', column_chosen_index, column_vector, preferred_e...  33.2 us
    all_gather x1, blocking collectives, on_device(): lax.all_gather(dir_half, 'row', axis=1, tiled=True)  33 us
  transfers between devices with their start and end apart: 2, of which 2 were waited for; matrix products, arithmetic and copies ran while one was open for 1% of the time, Pallas kernels for 0%

commit v1 on v0

v1 whole, which is shorter than its diff:
```python
import functools

import jax
import jax.numpy as jnp
from jax import lax
from jax.experimental import pallas as pl
from jax.experimental.pallas import tpu as pltpu
from jax.sharding import PartitionSpec as P

TILE = 128
FEATURES = 16
UNROLL = 4

AMPLITUDE = 0.025
NUGGET = 2.0
RADIUS = 1.0
HIGHEST = lax.Precision.HIGHEST


def cross_gram_matrix(former, latter):
    return lax.dot_general(
        former,
        latter,
        (((1,), (1,)), ((), ())),
        precision=HIGHEST,
        preferred_element_type=jnp.float32,
    )


def apply_left(matrix, vectors):
    return jnp.dot(matrix.T, vectors, precision=HIGHEST)


def symmetric_solve(matrix, target):
    balanced = 0.5 * (matrix + matrix.T)
    factor = jnp.linalg.cholesky(balanced)
    middle = lax.linalg.triangular_solve(factor, target, left_side=True, lower=True)
    return lax.linalg.triangular_solve(factor, middle, left_side=True, lower=True, transpose_a=True)


def split_three(value):
    high = lax.reduce_precision(value, 8, 7)
    rest = value - high
    middle = lax.reduce_precision(rest, 8, 7)
    return high, middle, rest - middle


def features(positions):
    coord = positions.astype(jnp.float32)
    x, y = coord[0], coord[1]
    high, middle, low = split_three(x * x + y * y)
    one = jnp.ones_like(x)
    zero = jnp.zeros_like(x)
    pad = [zero] * (FEATURES - 8)
    near = jnp.stack([x, y, high, middle, low, one, one, one] + pad)
    far = 16.0 * jnp.stack([-2.0 * x, -2.0 * y, one, one, one, high, middle, low] + pad)
    return near.astype(jnp.bfloat16), far.astype(jnp.bfloat16)


def kernel_of(square):
    square = jnp.minimum(jnp.maximum(square, 1e-20), 16.0)
    quad = square * lax.rsqrt(square)
    remain = 4.0 - quad
    remain = remain * remain
    return (remain * remain * (quad + 1.0)).astype(jnp.bfloat16)


def pair_kernel(
    own_tiles, pairs, count, near, far, row_vec, col_vec, row_out, col_out, own_out, row_acc, col_acc
):
    row_acc[...] = jnp.zeros_like(row_acc)
    col_acc[...] = jnp.zeros_like(col_acc)
    scale = AMPLITUDE / 256.0
    live = count[0]

    def products(i, j):
        block = kernel_of(jnp.dot(near[i], far[j], preferred_element_type=jnp.float32))
        forward = lax.dot_general(
            col_vec[j], block, (((1,), (1,)), ((), ())), preferred_element_type=jnp.float32
        )
        backward = jnp.dot(row_vec[i], block, preferred_element_type=jnp.float32)
        return forward, backward

    def several(first, number):
        index = [(pairs[0, first + k], pairs[1, first + k]) for k in range(number)]
        results = [products(i, j) for i, j in index]
        for (i, j), (forward, backward) in zip(index, results):
            row_acc[i] += forward
            col_acc[j] += backward

    whole = live // UNROLL

    @pl.loop(0, whole)
    def _(step):
        several(step * UNROLL, UNROLL)

    @pl.loop(whole * UNROLL, live)
    def _(slot):
        several(slot, 1)

    row_base = lax.axis_index("col") * own_tiles
    col_base = lax.axis_index("row") * own_tiles

    @pl.loop(0, own_tiles)
    def _(t):
        block = kernel_of(
            jnp.dot(near[row_base + t], far[col_base + t], preferred_element_type=jnp.float32)
        )
        own_out[t] = scale * lax.dot_general(
            col_vec[col_base + t],
            block,
            (((1,), (1,)), ((), ())),
            preferred_element_type=jnp.float32,
        )

    row_out[...] = (scale * row_acc[...]).astype(row_out.dtype)
    col_out[...] = (scale * col_acc[...]).astype(col_out.dtype)


def tile_major(array):
    rows, points = array.shape
    return array.reshape(rows, points // TILE, TILE).transpose(1, 0, 2)


def on_device(solution_field, residual, direction, positions, tile_pairs, pair_count):
    probes, own_points = direction.shape
    own_tiles = own_points // TILE
    own_vec = tile_major(direction.astype(jnp.bfloat16))
    near, far = features(positions)
    near = near.reshape(FEATURES, own_tiles, TILE).transpose(1, 2, 0)
    packed = jnp.concatenate([own_vec, tile_major(far)], axis=1)
    col_pack = lax.all_gather(packed, "row", axis=0, tiled=True)
    col_vec, far = col_pack[:, :probes], col_pack[:, probes:]
    row_vec = lax.all_gather(own_vec, "col", axis=0, tiled=True)
    near = lax.all_gather(near, "col", axis=0, tiled=True)
    row_tiles, col_tiles = row_vec.shape[0], col_vec.shape[0]
    vmem = pl.BlockSpec(memory_space=pltpu.VMEM)
    smem = pl.BlockSpec(memory_space=pltpu.SMEM)
    row_part, col_part, own_product = pl.pallas_call(
        functools.partial(pair_kernel, own_tiles),
        out_shape=(
            jax.ShapeDtypeStruct((row_tiles, probes, TILE), jnp.bfloat16),
            jax.ShapeDtypeStruct((col_tiles, probes, TILE), jnp.bfloat16),
            jax.ShapeDtypeStruct((own_tiles, probes, TILE), jnp.float32),
        ),
        in_specs=[smem, smem, vmem, vmem, vmem, vmem],
        out_specs=(vmem, vmem, vmem),
        scratch_shapes=[
            pltpu.VMEM((row_tiles, probes, TILE), jnp.float32),
            pltpu.VMEM((col_tiles, probes, TILE), jnp.float32),
        ],
        name="pairs",
    )(tile_pairs, pair_count, near, far, row_vec, col_vec)
    row_part = lax.psum_scatter(row_part, "col", scatter_dimension=0, tiled=True)
    col_part = lax.psum_scatter(col_part, "row", scatter_dimension=0, tiled=True)
    product = own_product + row_part.astype(jnp.float32) + col_part.astype(jnp.float32)
    applied = NUGGET * direction + product.transpose(1, 0, 2).reshape(probes, own_points)
    curvature, crossing, norm_old, image_resid, square = lax.psum(
        (
            cross_gram_matrix(direction, applied),
            cross_gram_matrix(direction, residual),
            cross_gram_matrix(residual, residual),
            cross_gram_matrix(applied, residual),
            cross_gram_matrix(applied, applied),
        ),
        ("row", "col"),
    )
    step_size = symmetric_solve(curvature, crossing)
    residual_next = residual - apply_left(step_size, applied)
    shifted = jnp.dot(step_size.T, image_resid, precision=HIGHEST)
    quadratic = jnp.dot(
        step_size.T, jnp.dot(square, step_size, precision=HIGHEST), precision=HIGHEST
    )
    norm_new = norm_old - shifted - shifted.T + quadratic
    solution_next = solution_field + apply_left(step_size, direction)
    mix_weight = symmetric_solve(norm_old, norm_new)
    direction_next = residual_next + apply_left(mix_weight, direction)
    return (solution_next, residual_next, direction_next)


def solution(mesh):
    whole = P(None, ("row", "col"))
    return jax.shard_map(
        on_device,
        mesh=mesh,
        in_specs=(whole, whole, whole, whole, whole, P(("row", "col"))),
        out_specs=(whole, whole, whole),
        check_vma=False,
    )
```

time: 681 us -> 503 us (0.74)
  Pallas kernels: 0 us -> 292 us
  matrix products: 255 us -> 4.79 us
  other arithmetic: 159 us -> 15.1 us
  blocking collectives: 116 us -> 86.7 us
  waiting for transfers between devices: 106 us -> 83.8 us
  local copies, waits for them, and re-layouts: 24.3 us -> 4.47 us
    pallas_call x0 -> x1, Pallas kernels: none -> 292 us  [on_device(): pl.pallas_call(functools.partial(pair_kernel, own_tiles), out_shape=(jax....]
    dot_general x193 -> x0, matrix products: 251 us -> none  [the longest x24 83.6 us: stepped(): jnp.einsum('au,lax->lux', column_chosen_index.astype(jnp.float32), backwa...]
    psum x2 -> x0, waiting for transfers between devices: 106 us -> none  [the longest x1 76.2 us: on_device(): lax.psum(col_flat.astype(jnp.bfloat16), 'row').astype(jnp.float32)]
    reduce_scatter x0 -> x2, waiting for transfers between devices: none -> 83.1 us  [the longest x1 66.1 us: on_device(): lax.psum_scatter(col_part, 'row', scatter_dimension=0, tiled=True)]
    reduce_sum x25 -> x0, other arithmetic: 66.6 us -> none  [kernel_tile(): distance = jnp.sqrt(jnp.sum(differ * differ, axis=0)) / RADIUS]
    convert_element_type x27 -> x1, other arithmetic: 62.4 us -> 0.72 us  [features(): coord = positions.astype(jnp.float32)]
    all_gather x4 -> x3, blocking collectives: 74.9 us -> 45.6 us  [the longest x1 33.9 us: on_device(): col_pack = lax.all_gather(packed, 'row', axis=0, tiled=True)]
    slice x24 -> x2, local copies, waits for them, and re-layouts: 19.1 us -> 1.57 us  [on_device(): col_vec, far = (col_pack[:, :probes], col_pack[:, probes:])]
  transfers between devices with their start and end apart: 2 -> 2, of which waited for: 2 -> 2; matrix products, arithmetic and copies ran while one was open for 1% -> 0% of each run, Pallas kernels for 0% -> 0%
where the time goes in v1:
time: 503 us; the launch traced here: 502 us
  Pallas kernels  292 us (58%)
  blocking collectives  86.7 us (17%)
  waiting for transfers between devices  83.8 us (17%)
  other arithmetic  15.1 us (3%)
  between operations  15 us (3%)
    pallas_call x1, Pallas kernels, on_device(): pl.pallas_call(functools.partial(pair_kernel, own_tiles), out_shape=(jax....  292 us
    reduce_scatter x1, waiting for transfers between devices, on_device(): lax.psum_scatter(col_part, 'row', scatter_dimension=0, tiled=True)  66.1 us
    psum x1, blocking collectives, on_device(): lax.psum((cross_gram_matrix(direction, applied), cross_gram_matrix(direct...  41.1 us
    all_gather x1, blocking collectives, on_device(): col_pack = lax.all_gather(packed, 'row', axis=0, tiled=True)  33.9 us
    reduce_scatter x1, waiting for transfers between devices, on_device(): lax.psum_scatter(row_part, 'col', scatter_dimension=0, tiled=True)  17 us
  transfers between devices with their start and end apart: 2, of which 2 were waited for; matrix products, arithmetic and copies ran while one was open for 0% of the time, Pallas kernels for 0%

profile of v1, /device:TPU:0, one launch (start us, length us, event | category | flops | bytes accessed | tf_op | source)
XLA Modules:
  0.0 502.1 jit_solution(8789474579065366771)
XLA Ops:
  7.2 0.7 convert_element_type.18
  8.2 33.9 %all_gather.10 = bf16[64,48,128]{2,1,0:T(8,128)(2,1)S(1)} all-gather(bf16[8,48,128]{2,1,0:T(8,128)(2,1)S(1)} %copy.32), channel_id=1, replica_groups=mesh['row'=8,'col'=4] {'row'}, dimensions={0}, use_global_device_ids=true | all-gather | bytes 884736 | tf_op jit(solution)/shard_map/all_gather | solution.py:132
  42.1 0.9 slice.28.col_vec
  42.9 0.7 slice.27.far
  43.6 0.7 copy-done.5
  44.4 5.4 %all_gather.9 = bf16[32,128,16]{1,2,0:T(8,128)(2,1)S(1)} all-gather(bf16[8,128,16]{1,2,0:T(8,128)(2,1)S(1)} %bitcast.90), channel_id=1, replica_groups=mesh['row'=8,'col'=4] {'col'}, dimensions={0}, use_global_device_ids=true | all-gather | bytes 163840 | tf_op jit(solution)/shard_map/all_gather | solution.py:135
  49.8 1.3 copy.34.near
  51.2 6.3 %all_gather.11.row_vec = bf16[32,32,128]{2,1,0:T(8,128)(2,1)} all-gather(bf16[8,32,128]{2,1,0:T(8,128)(2,1)S(1)} %copy.33), channel_id=1, replica_groups=mesh['row'=8,'col'=4] {'col'}, dimensions={0}, use_global_device_ids=true | all-gather | bytes 327680 | tf_op jit(solution)/shard_map/all_gather | solution.py:134
  58.1 292.2 %pairs.2 = (bf16[32,32,128]{2,1,0:T(8,128)(2,1)}, bf16[64,32,128]{2,1,0:T(8,128)(2,1)}, f32[8,32,128]{2,1,0:T(8,128)}) custom-call(s32[2,1536]{1,0:T(2,128)} %pairs.3, s32[1]{0:T(128)S(6)} %copy.67.count, bf16[32,128,16]{2,1,0:T(8,128)(2,1)} %copy.34.near, bf16[64,16,128]{2,1,0:T(8,128)(2,1)} %slice.27.far, bf16[32,32,128]{2,1,0:T(8,128)(2,1)} %all_gather.11.row_vec, ...), custom_call_target="tpu_custom_call" | custom-call | tf_op jit(solution)/shard_map/pairs/pallas_call | solution.py:139
  350.4 0.7 reduce-scatter.5.cloned.1.call-update
  351.8 17.0 %reduce-scatter.3.cloned.1.call-done = bf16[8,32,128]{2,1,0:T(8,128)(2,1)} async-done(((bf16[32,32,128]{2,1,0:T(8,128)(2,1)}), bf16[8,32,128]{2,1,0:T(8,128)(2,1)}) %reduce-scatter.3.cloned.1.call-update) | async-done | bytes 65552 | tf_op jit(solution)/shard_map/reduce_scatter | solution.py:154
  368.8 66.1 %reduce-scatter.5.cloned.1.call-done = bf16[8,32,128]{2,1,0:T(8,128)(2,1)} async-done(((bf16[64,32,128]{2,1,0:T(8,128)(2,1)}), bf16[8,32,128]{2,1,0:T(8,128)(2,1)}) %reduce-scatter.5.cloned.1.call-update) | async-done | bytes 65552 | tf_op jit(solution)/shard_map/reduce_scatter | solution.py:155
  434.9 0.9 add_bitcast_fusion
  436.6 41.1 %all-reduce = (f32[32,32]{1,0:T(8,128)S(1)}, f32[32,32]{1,0:T(8,128)S(1)}, f32[32,32]{1,0:T(8,128)S(1)}, f32[32,32]{1,0:T(8,128)S(1)}, f32[32,32]{1,0:T(8,128)S(1)}) all-reduce(f32[32,32]{1,0:T(8,128)S(1)} %fusion.17, f32[32,32]{1,0:T(8,128)S(1)} %convolution_bitcast_fusion, ...), channel_id=1, replica_groups=mesh['row'=8,'col'=4] {'row','col'}, use_global_device_ids=true, to_apply=%region_5.7 | all-reduce | flops 5120 | bytes 40960 | tf_op jit(solution)/shard_map/psum | solution.py:158
  477.9 2.9 cholesky.55
  480.9 0.6 compare_reduce_fusion
  481.5 0.7 fusion.2
  482.2 2.4 custom-call.13
  484.7 2.9 cholesky.44
  487.7 0.6 compare_reduce_fusion.1
  488.3 0.7 fusion.1
  489.0 2.4 custom-call.11
  493.4 1.0 convolution_add_fusion.1
  494.3 1.0 convolution_add_fusion
  (61 shorter events, 4.0 us)
Async XLA Ops:
  7.2 0.9 copy-start
  7.2 361.6 %reduce-scatter.3.cloned.1.call-start = ((), (), s32[]{:S(2)}) async-start(), calls=%async_computation.2 | async-start | bytes 327680 | tf_op jit(solution)/shard_map/reduce_scatter | solution.py:154
  43.6 0.7 copy-start.5
  350.4 84.5 %reduce-scatter.5.cloned.1.call-start = ((), (), s32[]{:S(2)}) async-start(), calls=%async_computation.3 | async-start | bytes 589824 | tf_op jit(solution)/shard_map/reduce_scatter | solution.py:155
  350.4 0.9 copy-start.1
  351.5 83.4 %copy-start.4 = (f32[8,32,128]{2,1,0:T(8,128)S(1)}, f32[8,32,128]{2,1,0:T(8,128)}, u32[]{:S(2)}) copy-start(f32[8,32,128]{2,1,0:T(8,128)} %get-tuple-element.9) | copy-start | bytes 393220
  492.1 2.2 copy-start.2
  492.4 0.9 copy-start.3
Sparse Core Ops, SparseCore 0:
  350.5 18.2 reduce-scatter.2
  372.2 62.6 reduce-scatter.4

commit v2 on v1

--- a/solution.py
+++ b/solution.py
@@ -1,5 +1,3 @@
-import functools
-
 import jax
 import jax.numpy as jnp
 from jax import lax
@@ -9,7 +7,8 @@
 
 TILE = 128
 FEATURES = 16
-UNROLL = 4
+UNROLL = 2
+BLOCK = 2 * TILE
 
 AMPLITUDE = 0.025
 NUGGET = 2.0
@@ -57,97 +56,122 @@
     return near.astype(jnp.bfloat16), far.astype(jnp.bfloat16)
 
 
-def kernel_of(square):
-    square = jnp.minimum(jnp.maximum(square, 1e-20), 16.0)
+def kernel_of(square, floor):
+    square = jnp.minimum(jnp.maximum(square, floor), 16.0)
     quad = square * lax.rsqrt(square)
     remain = 4.0 - quad
     remain = remain * remain
     return (remain * remain * (quad + 1.0)).astype(jnp.bfloat16)
 
 
+def block_of(near, far, floors):
+    square = jnp.dot(near, far, preferred_element_type=jnp.float32)
+    rows = []
+    for a in range(2):
+        part = square[a * TILE : (a + 1) * TILE]
+        row = [kernel_of(part[:, b * TILE : (b + 1) * TILE], floors[a][b]) for b in range(2)]
+        rows.append(jnp.concatenate(row, axis=1))
+    return jnp.concatenate(rows, axis=0)
+
+
+def times_transposed(vectors, block):
+    return lax.dot_general(
+        vectors, block, (((1,), (1,)), ((), ())), preferred_element_type=jnp.float32
+    )
+
+
 def pair_kernel(
-    own_tiles, pairs, count, near, far, row_vec, col_vec, row_out, col_out, own_out, row_acc, col_acc
+    pairs, count, near, far, row_vec, col_vec, row_out, col_out, own_out, col_acc, floor
 ):
-    row_acc[...] = jnp.zeros_like(row_acc)
-    col_acc[...] = jnp.zeros_like(col_acc)
+    row_blocks, col_blocks = near.shape[0], far.shape[0]
+    own_blocks = own_out.shape[0]
+    stride = 2 * col_blocks
     scale = AMPLITUDE / 256.0
     live = count[0]
+    col_acc[...] = jnp.zeros_like(col_acc)
+
+    @pl.loop(0, 2 * row_blocks * stride // 16)
+    def _(step):
+        for k in range(16):
+            floor[step * 16 + k] = 16.0
+
+    def mark(slot):
+        floor[pairs[0, slot] * stride + pairs[1, slot]] = 1e-20
+
+    whole = live // 8
+
+    @pl.loop(0, whole)
+    def _(step):
+        for k in range(8):
+            mark(step * 8 + k)
+
+    @pl.loop(whole * 8, live)
+    def _(slot):
+        mark(slot)
 
     def products(i, j):
-        block = kernel_of(jnp.dot(near[i], far[j], preferred_element_type=jnp.float32))
-        forward = lax.dot_general(
-            col_vec[j], block, (((1,), (1,)), ((), ())), preferred_element_type=jnp.float32
-        )
+        base = 2 * i * stride + 2 * j
+        floors = [[floor[base + a * stride + b] for b in range(2)] for a in range(2)]
+        block = block_of(near[i], far[j], floors)
+        forward = times_transposed(col_vec[j], block)
         backward = jnp.dot(row_vec[i], block, preferred_element_type=jnp.float32)
         return forward, backward
 
-    def several(first, number):
-        index = [(pairs[0, first + k], pairs[1, first + k]) for k in range(number)]
-        results = [products(i, j) for i, j in index]
-        for (i, j), (forward, backward) in zip(index, results):
-            row_acc[i] += forward
-            col_acc[j] += backward
-
-    whole = live // UNROLL
-
-    @pl.loop(0, whole)
-    def _(step):
-        several(step * UNROLL, UNROLL)
-
-    @pl.loop(whole * UNROLL, live)
-    def _(slot):
-        several(slot, 1)
-
-    row_base = lax.axis_index("col") * own_tiles
-    col_base = lax.axis_index("row") * own_tiles
-
-    @pl.loop(0, own_tiles)
+    @pl.loop(0, row_blocks)
+    def _(i):
+        def several(step, total):
+            results = [products(i, step * UNROLL + k) for k in range(UNROLL)]
+            for k, (forward, backward) in enumerate(results):
+                total = total + forward
+                col_acc[step * UNROLL + k] += backward
+            return total
+
+        start = jnp.zeros(row_vec.shape[1:], jnp.float32)
+        total = lax.fori_loop(0, col_blocks // UNROLL, several, start)
+        row_out[i] = (scale * total).astype(row_out.dtype)
+
+    row_base = lax.axis_index("col") * own_blocks
+    col_base = lax.axis_index("row") * own_blocks
+
+    @pl.loop(0, own_blocks)
     def _(t):
-        block = kernel_of(
-            jnp.dot(near[row_base + t], far[col_base + t], preferred_element_type=jnp.float32)
-        )
-        own_out[t] = scale * lax.dot_general(
-            col_vec[col_base + t],
-            block,
-            (((1,), (1,)), ((), ())),
-            preferred_element_type=jnp.float32,
-        )
-
-    row_out[...] = (scale * row_acc[...]).astype(row_out.dtype)
+        block = block_of(near[row_base + t], far[col_base + t], [[1e-20, 16.0], [16.0, 1e-20]])
+        own_out[t] = scale * times_transposed(col_vec[col_base + t], block)
+
     col_out[...] = (scale * col_acc[...]).astype(col_out.dtype)
 
 
-def tile_major(array):
+def block_major(array):
     rows, points = array.shape
-    return array.reshape(rows, points // TILE, TILE).transpose(1, 0, 2)
+    return array.reshape(rows, points // BLOCK, BLOCK).transpose(1, 0, 2)
 
 
 def on_device(solution_field, residual, direction, positions, tile_pairs, pair_count):
     probes, own_points = direction.shape
-    own_tiles = own_points // TILE
-    own_vec = tile_major(direction.astype(jnp.bfloat16))
+    own_blocks = own_points // BLOCK
+    own_vec = block_major(direction.astype(jnp.bfloat16))
     near, far = features(positions)
-    near = near.reshape(FEATURES, own_tiles, TILE).transpose(1, 2, 0)
-    packed = jnp.concatenate([own_vec, tile_major(far)], axis=1)
+    near = near.reshape(FEATURES, own_blocks, BLOCK).transpose(1, 2, 0)
+    packed = jnp.concatenate([own_vec, block_major(far)], axis=1)
     col_pack = lax.all_gather(packed, "row", axis=0, tiled=True)
     col_vec, far = col_pack[:, :probes], col_pack[:, probes:]
     row_vec = lax.all_gather(own_vec, "col", axis=0, tiled=True)
     near = lax.all_gather(near, "col", axis=0, tiled=True)
-    row_tiles, col_tiles = row_vec.shape[0], col_vec.shape[0]
+    row_blocks, col_blocks = row_vec.shape[0], col_vec.shape[0]
     vmem = pl.BlockSpec(memory_space=pltpu.VMEM)
     smem = pl.BlockSpec(memory_space=pltpu.SMEM)
     row_part, col_part, own_product = pl.pallas_call(
-        functools.partial(pair_kernel, own_tiles),
+        pair_kernel,
         out_shape=(
-            jax.ShapeDtypeStruct((row_tiles, probes, TILE), jnp.bfloat16),
-            jax.ShapeDtypeStruct((col_tiles, probes, TILE), jnp.bfloat16),
-            jax.ShapeDtypeStruct((own_tiles, probes, TILE), jnp.float32),
+            jax.ShapeDtypeStruct((row_blocks, probes, BLOCK), jnp.bfloat16),
+            jax.ShapeDtypeStruct((col_blocks, probes, BLOCK), jnp.bfloat16),
+            jax.ShapeDtypeStruct((own_blocks, probes, BLOCK), jnp.float32),
         ),
         in_specs=[smem, smem, vmem, vmem, vmem, vmem],
         out_specs=(vmem, vmem, vmem),
         scratch_shapes=[
-            pltpu.VMEM((row_tiles, probes, TILE), jnp.float32),
-            pltpu.VMEM((col_tiles, probes, TILE), jnp.float32),
+            pltpu.VMEM((col_blocks, probes, BLOCK), jnp.float32),
+            pltpu.SMEM((4 * row_blocks * col_blocks,), jnp.float32),
         ],
         name="pairs",
     )(tile_pairs, pair_count, near, far, row_vec, col_vec)

time: 503 us -> 343 us (0.68)
  Pallas kernels: 292 us -> 126 us
  waiting for transfers between devices: 83.8 us -> 89.7 us
    pallas_call x1, Pallas kernels: 292 us -> 126 us  [on_device(): pl.pallas_call(pair_kernel, out_shape=(jax.ShapeDtypeStruct((row_blocks,...]
    reduce_scatter x1, waiting for transfers between devices: 17 us -> 22.8 us  [on_device(): lax.psum_scatter(row_part, 'col', scatter_dimension=0, tiled=True)]
where the time goes in v2:
time: 343 us
  Pallas kernels  126 us (37%)
  waiting for transfers between devices  89.7 us (26%)
  blocking collectives  86.8 us (25%)
  other arithmetic  15.2 us (4%)
  between operations  15 us (4%)
  local copies, waits for them, and re-layouts  5.26 us (2%)
  matrix products  4.78 us (1%)
    pallas_call x1, Pallas kernels, on_device(): pl.pallas_call(pair_kernel, out_shape=(jax.ShapeDtypeStruct((row_blocks,...  126 us
    reduce_scatter x1, waiting for transfers between devices, on_device(): lax.psum_scatter(col_part, 'row', scatter_dimension=0, tiled=True)  66.1 us
    psum x1, blocking collectives, on_device(): lax.psum((cross_gram_matrix(direction, applied), cross_gram_matrix(direct...  41.3 us
    all_gather x1, blocking collectives, on_device(): col_pack = lax.all_gather(packed, 'row', axis=0, tiled=True)  33.9 us
    reduce_scatter x1, waiting for transfers between devices, on_device(): lax.psum_scatter(row_part, 'col', scatter_dimension=0, tiled=True)  22.8 us
    another operation x6, other arithmetic, symmetric_solve(): factor = jnp.linalg.cholesky(balanced)  7.2 us
  transfers between devices with their start and end apart: 2, of which 2 were waited for; matrix products, arithmetic and copies ran while one was open for 0% of the time, Pallas kernels for 0%

profile of v2, /device:TPU:0, one launch (start us, length us, event | category | flops | bytes accessed | tf_op | source)
XLA Modules:
  0.0 343.3 jit_solution(5004761146732037989)
XLA Ops:
  7.2 0.7 convert_element_type.18
  8.2 0.7 copy-done
  9.0 33.9 %all_gather.10 = bf16[32,48,256]{2,1,0:T(8,128)(2,1)S(1)} all-gather(bf16[4,48,256]{2,1,0:T(8,128)(2,1)S(1)} %copy.34), channel_id=1, replica_groups=mesh['row'=8,'col'=4] {'row'}, dimensions={0}, use_global_device_ids=true | all-gather | bytes 884736 | tf_op jit(solution)/shard_map/all_gather | solution.py:156
  42.9 0.9 slice.28.col_vec
  43.7 0.7 slice.27.far
  44.6 0.7 copy-done.5
  45.3 5.4 %all_gather.9 = bf16[16,256,16]{1,2,0:T(8,128)(2,1)S(1)} all-gather(bf16[4,256,16]{1,2,0:T(8,128)(2,1)S(1)} %bitcast.76), channel_id=1, replica_groups=mesh['row'=8,'col'=4] {'col'}, dimensions={0}, use_global_device_ids=true | all-gather | bytes 163840 | tf_op jit(solution)/shard_map/all_gather | solution.py:159
  50.7 1.3 copy.36.near
  52.0 6.3 %all_gather.11.row_vec = bf16[16,32,256]{2,1,0:T(8,128)(2,1)} all-gather(bf16[4,32,256]{2,1,0:T(8,128)(2,1)S(1)} %copy.35), channel_id=1, replica_groups=mesh['row'=8,'col'=4] {'col'}, dimensions={0}, use_global_device_ids=true | all-gather | bytes 327680 | tf_op jit(solution)/shard_map/all_gather | solution.py:158
  59.0 126.5 %pairs.2 = (bf16[16,32,256]{2,1,0:T(8,128)(2,1)}, bf16[32,32,256]{2,1,0:T(8,128)(2,1)}, f32[4,32,256]{2,1,0:T(8,128)}) custom-call(s32[2,1536]{1,0:T(2,128)} %pairs.3, s32[1]{0:T(128)S(6)} %copy.53.count, bf16[16,256,16]{2,1,0:T(8,128)(2,1)} %copy.36.near, bf16[32,16,256]{2,1,0:T(8,128)(2,1)} %slice.27.far, bf16[16,32,256]{2,1,0:T(8,128)(2,1)} %all_gather.11.row_vec, ...), custom_call_target="tpu_custom_call" | custom-call | tf_op jit(solution)/shard_map/pairs/pallas_call | solution.py:163
  185.5 0.7 reduce-scatter.5.cloned.1.call-update
  186.9 22.8 %reduce-scatter.3.cloned.1.call-done = bf16[4,32,256]{2,1,0:T(8,128)(2,1)} async-done(((bf16[16,32,256]{2,1,0:T(8,128)(2,1)}), bf16[4,32,256]{2,1,0:T(8,128)(2,1)}) %reduce-scatter.3.cloned.1.call-update) | async-done | bytes 65552 | tf_op jit(solution)/shard_map/reduce_scatter | solution.py:178
  209.8 66.1 %reduce-scatter.5.cloned.1.call-done = bf16[4,32,256]{2,1,0:T(8,128)(2,1)} async-done(((bf16[32,32,256]{2,1,0:T(8,128)(2,1)}), bf16[4,32,256]{2,1,0:T(8,128)(2,1)}) %reduce-scatter.5.cloned.1.call-update) | async-done | bytes 65552 | tf_op jit(solution)/shard_map/reduce_scatter | solution.py:179
  275.9 0.9 add_bitcast_fusion
  277.6 41.3 %all-reduce = (f32[32,32]{1,0:T(8,128)S(1)}, f32[32,32]{1,0:T(8,128)S(1)}, f32[32,32]{1,0:T(8,128)S(1)}, f32[32,32]{1,0:T(8,128)S(1)}, f32[32,32]{1,0:T(8,128)S(1)}) all-reduce(f32[32,32]{1,0:T(8,128)S(1)} %fusion.18, f32[32,32]{1,0:T(8,128)S(1)} %convolution_bitcast_fusion, ...), channel_id=1, replica_groups=mesh['row'=8,'col'=4] {'row','col'}, use_global_device_ids=true, to_apply=%region_5.7 | all-reduce | flops 5120 | bytes 40960 | tf_op jit(solution)/shard_map/psum | solution.py:182
  319.1 2.9 cholesky.55
  322.7 0.7 fusion.2
  323.4 2.4 custom-call.13
  325.9 2.9 cholesky.44
  328.9 0.6 compare_reduce_fusion.1
  329.5 0.7 fusion.1
  330.2 2.4 custom-call.11
  334.5 1.0 convolution_add_fusion.1
  335.5 1.0 convolution_add_fusion
  (66 shorter events, 4.9 us)
Async XLA Ops:
  7.2 202.6 %reduce-scatter.3.cloned.1.call-start = ((), (), s32[]{:S(2)}) async-start(), calls=%async_computation.2 | async-start | bytes 327680 | tf_op jit(solution)/shard_map/reduce_scatter | solution.py:178
  7.9 0.9 copy-start
  44.5 0.7 copy-start.5
  185.5 90.4 %reduce-scatter.5.cloned.1.call-start = ((), (), s32[]{:S(2)}) async-start(), calls=%async_computation.3 | async-start | bytes 589824 | tf_op jit(solution)/shard_map/reduce_scatter | solution.py:179
  185.5 0.9 copy-start.1
  186.7 89.3 %copy-start.4 = (f32[4,32,256]{2,1,0:T(8,128)S(1)}, f32[4,32,256]{2,1,0:T(8,128)}, u32[]{:S(2)}) copy-start(f32[4,32,256]{2,1,0:T(8,128)} %get-tuple-element.9) | copy-start | bytes 393220
  333.3 2.2 copy-start.2
  333.6 0.9 copy-start.3
Sparse Core Ops, SparseCore 0:
  185.6 24.1 reduce-scatter.2
  213.1 62.7 reduce-scatter.4

commit v3 on v2

--- a/solution.py
+++ b/solution.py
@@ -1,3 +1,5 @@
+import functools
+
 import jax
 import jax.numpy as jnp
 from jax import lax
@@ -141,6 +143,141 @@
     col_out[...] = (scale * col_acc[...]).astype(col_out.dtype)
 
 
+MESH = pl.DeviceIdType.MESH
+
+
+def greet(sizes):
+    barrier = pltpu.get_barrier_semaphore()
+    for axis, size in sizes:
+        me = lax.axis_index(axis)
+        for k in range(1, size):
+            peer = lax.rem(me + k, size)
+            pl.semaphore_signal(barrier, inc=1, device_id={axis: peer}, device_id_type=MESH)
+    pl.semaphore_wait(barrier, sum(size - 1 for _, size in sizes))
+
+
+class Exchange:
+    def __init__(self, axis, size, source, landing, send_sem, recv_sem):
+        self.axis, self.size, self.source, self.landing = axis, size, source, landing
+        self.send_sem, self.recv_sem = send_sem, recv_sem
+        self.me = lax.axis_index(axis)
+
+    def copy(self, k, source, slot, peer):
+        return pltpu.make_async_remote_copy(
+            src_ref=source,
+            dst_ref=self.landing.at[slot],
+            send_sem=self.send_sem.at[k],
+            recv_sem=self.recv_sem.at[k],
+            device_id={self.axis: peer},
+            device_id_type=MESH,
+        )
+
+    def outgoing(self, k):
+        peer = lax.rem(self.me + k, self.size)
+        return self.copy(k, self.source(peer), self.me, peer)
+
+    def start(self):
+        for k in range(1, self.size):
+            self.outgoing(k).start()
+
+    def wait_recv(self):
+        for k in range(1, self.size):
+            origin = lax.rem(self.me + self.size - k, self.size)
+            self.copy(k, self.landing.at[origin], origin, origin).wait_recv()
+
+    def wait_send(self):
+        for k in range(1, self.size):
+            self.outgoing(k).wait_send()
+
+
+def gather_kernel(
+    n_row, n_col, row_in, col_in, row_out, col_out, own_sem, row_send, row_recv, col_send, col_recv
+):
+    row_me, col_me = lax.axis_index("col"), lax.axis_index("row")
+    own = [
+        pltpu.make_async_copy(row_in, row_out.at[row_me], own_sem.at[0]),
+        pltpu.make_async_copy(col_in, col_out.at[col_me], own_sem.at[1]),
+    ]
+    for copy in own:
+        copy.start()
+    greet((("row", n_row), ("col", n_col)))
+    over_row = Exchange("row", n_row, lambda peer: col_in, col_out, col_send, col_recv)
+    over_col = Exchange("col", n_col, lambda peer: row_in, row_out, row_send, row_recv)
+    over_row.start()
+    over_col.start()
+    for copy in own:
+        copy.wait()
+    for exchange in (over_col, over_row):
+        exchange.wait_recv()
+        exchange.wait_send()
+
+
+def image_kernel(
+    n_row,
+    n_col,
+    row_part,
+    col_part,
+    own_product,
+    direction,
+    residual,
+    applied,
+    gram,
+    row_land,
+    col_land,
+    gram_own,
+    gram_half,
+    gram_col,
+    gram_row,
+    *sems,
+):
+    blocks = own_product.shape[0]
+    row_me, col_me = lax.axis_index("col"), lax.axis_index("row")
+    greet((("row", n_row), ("col", n_col)))
+
+    def part_of(parts):
+        return lambda peer: parts.at[pl.ds(peer * blocks, blocks)]
+
+    over_row = Exchange("row", n_row, part_of(col_part), col_land, sems[0], sems[1])
+    over_col = Exchange("col", n_col, part_of(row_part), row_land, sems[2], sems[3])
+    over_row.start()
+    over_col.start()
+    total = own_product[...]
+    total += row_part[pl.ds(row_me * blocks, blocks)].astype(jnp.float32)
+    total += col_part[pl.ds(col_me * blocks, blocks)].astype(jnp.float32)
+    over_col.wait_recv()
+    for k in range(1, n_col):
+        total += row_land[lax.rem(row_me + k, n_col)].astype(jnp.float32)
+    over_row.wait_recv()
+    for k in range(1, n_row):
+        total += col_land[lax.rem(col_me + k, n_row)].astype(jnp.float32)
+    flat = jnp.concatenate([total[b] for b in range(blocks)], axis=1)
+    image = NUGGET * direction[...] + flat
+    applied[...] = image
+    left = jnp.concatenate([image, residual[...]], axis=0)
+    right = jnp.concatenate([left, direction[...]], axis=0)
+    product = cross_gram_matrix(left, right)
+    lanes = gram_own.shape[1] - product.shape[1]
+    gram_own[...] = jnp.concatenate(
+        [product, jnp.zeros((product.shape[0], lanes), jnp.float32)], axis=1
+    )
+    gram_over_col = Exchange("col", n_col, lambda peer: gram_own, gram_col, sems[4], sems[5])
+    gram_over_col.start()
+    gram_over_col.wait_recv()
+    half = gram_own[...]
+    for k in range(1, n_col):
+        half += gram_col[lax.rem(row_me + k, n_col)]
+    gram_half[...] = half
+    gram_over_row = Exchange("row", n_row, lambda peer: gram_half, gram_row, sems[6], sems[7])
+    gram_over_row.start()
+    gram_over_row.wait_recv()
+    whole = gram_half[...]
+    for k in range(1, n_row):
+        whole += gram_row[lax.rem(col_me + k, n_row)]
+    gram[...] = whole
+    for exchange in (over_row, over_col, gram_over_col, gram_over_row):
+        exchange.wait_send()
+
+
 def block_major(array):
     rows, points = array.shape
     return array.reshape(rows, points // BLOCK, BLOCK).transpose(1, 0, 2)
@@ -151,15 +288,30 @@
     own_blocks = own_points // BLOCK
     own_vec = block_major(direction.astype(jnp.bfloat16))
     near, far = features(positions)
-    near = near.reshape(FEATURES, own_blocks, BLOCK).transpose(1, 2, 0)
-    packed = jnp.concatenate([own_vec, block_major(far)], axis=1)
-    col_pack = lax.all_gather(packed, "row", axis=0, tiled=True)
-    col_vec, far = col_pack[:, :probes], col_pack[:, probes:]
-    row_vec = lax.all_gather(own_vec, "col", axis=0, tiled=True)
-    near = lax.all_gather(near, "col", axis=0, tiled=True)
-    row_blocks, col_blocks = row_vec.shape[0], col_vec.shape[0]
+    n_row, n_col = lax.axis_size("row"), lax.axis_size("col")
     vmem = pl.BlockSpec(memory_space=pltpu.VMEM)
     smem = pl.BlockSpec(memory_space=pltpu.SMEM)
+    hbm = pl.BlockSpec(memory_space=pl.ANY)
+    row_sem, col_sem = pltpu.SemaphoreType.DMA((n_col,)), pltpu.SemaphoreType.DMA((n_row,))
+    row_in = jnp.concatenate([own_vec, block_major(near)], axis=1)
+    col_in = jnp.concatenate([own_vec, block_major(far)], axis=1)
+    row_pack, col_pack = pl.pallas_call(
+        functools.partial(gather_kernel, n_row, n_col),
+        out_shape=(
+            jax.ShapeDtypeStruct((n_col, *row_in.shape), jnp.bfloat16),
+            jax.ShapeDtypeStruct((n_row, *col_in.shape), jnp.bfloat16),
+        ),
+        in_specs=[vmem, vmem],
+        out_specs=(hbm, hbm),
+        scratch_shapes=[pltpu.SemaphoreType.DMA((2,)), row_sem, row_sem, col_sem, col_sem],
+        compiler_params=pltpu.CompilerParams(collective_id=0, has_side_effects=True),
+        name="gather",
+    )(row_in, col_in)
+    row_pack = row_pack.reshape(-1, *row_in.shape[1:])
+    col_pack = col_pack.reshape(-1, *col_in.shape[1:])
+    row_vec, near = row_pack[:, :probes], row_pack[:, probes:].transpose(0, 2, 1)
+    col_vec, far = col_pack[:, :probes], col_pack[:, probes:]
+    row_blocks, col_blocks = row_vec.shape[0], col_vec.shape[0]
     row_part, col_part, own_product = pl.pallas_call(
         pair_kernel,
         out_shape=(
@@ -175,20 +327,37 @@
         ],
         name="pairs",
     )(tile_pairs, pair_count, near, far, row_vec, col_vec)
-    row_part = lax.psum_scatter(row_part, "col", scatter_dimension=0, tiled=True)
-    col_part = lax.psum_scatter(col_part, "row", scatter_dimension=0, tiled=True)
-    product = own_product + row_part.astype(jnp.float32) + col_part.astype(jnp.float32)
-    applied = NUGGET * direction + product.transpose(1, 0, 2).reshape(probes, own_points)
-    curvature, crossing, norm_old, image_resid, square = lax.psum(
-        (
-            cross_gram_matrix(direction, applied),
-            cross_gram_matrix(direction, residual),
-            cross_gram_matrix(residual, residual),
-            cross_gram_matrix(applied, residual),
-            cross_gram_matrix(applied, applied),
+    applied, gram = pl.pallas_call(
+        functools.partial(image_kernel, n_row, n_col),
+        out_shape=(
+            jax.ShapeDtypeStruct((probes, own_points), jnp.float32),
+            jax.ShapeDtypeStruct((2 * probes, TILE), jnp.float32),
         ),
-        ("row", "col"),
-    )
+        in_specs=[vmem] * 5,
+        out_specs=(vmem, vmem),
+        scratch_shapes=[
+            pltpu.VMEM((n_col, *own_product.shape), jnp.bfloat16),
+            pltpu.VMEM((n_row, *own_product.shape), jnp.bfloat16),
+            pltpu.VMEM((2 * probes, TILE), jnp.float32),
+            pltpu.VMEM((2 * probes, TILE), jnp.float32),
+            pltpu.VMEM((n_col, 2 * probes, TILE), jnp.float32),
+            pltpu.VMEM((n_row, 2 * probes, TILE), jnp.float32),
+            col_sem,
+            col_sem,
+            row_sem,
+            row_sem,
+            row_sem,
+            row_sem,
+            col_sem,
+            col_sem,
+        ],
+        compiler_params=pltpu.CompilerParams(collective_id=1, has_side_effects=True),
+        name="image",
+    )(row_part, col_part, own_product, direction, residual)
+    square, image_resid = gram[:probes, :probes], gram[:probes, probes : 2 * probes]
+    norm_old = gram[probes:, probes : 2 * probes]
+    curvature = gram[:probes, 2 * probes : 3 * probes].T
+    crossing = gram[probes:, 2 * probes : 3 * probes].T
     step_size = symmetric_solve(curvature, crossing)
     residual_next = residual - apply_left(step_size, applied)
     shifted = jnp.dot(step_size.T, image_resid, precision=HIGHEST)

time: 343 us -> 210 us (0.61)
  waiting for transfers between devices: 89.7 us -> 0 us
  blocking collectives: 86.8 us -> 0 us
  Pallas kernels: 126 us -> 181 us
  between operations: 15 us -> 1.56 us
  local copies, waits for them, and re-layouts: 5.26 us -> 8.72 us
    reduce_scatter x2 -> x0, waiting for transfers between devices: 89 us -> none  [the longest x1 66.1 us: on_device(): lax.psum_scatter(col_part, 'row', scatter_dimension=0, tiled=True)]
    pallas_call x0 -> x2, Pallas kernels: none -> 48.5 us  [the longest x1 28.4 us: on_device(): pl.pallas_call(functools.partial(image_kernel, n_row, n_col), out_shape=(...]
    all_gather x3 -> x0, blocking collectives: 45.6 us -> none  [the longest x1 33.9 us: on_device(): col_pack = lax.all_gather(packed, 'row', axis=0, tiled=True)]
    psum x1 -> x0, blocking collectives: 41.3 us -> none  [on_device(): lax.psum((cross_gram_matrix(direction, applied), cross_gram_matrix(direct...]
    pallas_call x1, Pallas kernels: 126 us -> 132 us  [on_device(): pl.pallas_call(pair_kernel, out_shape=(jax.ShapeDtypeStruct((row_blocks,...]
  transfers between devices with their start and end apart: 2 -> 0, of which waited for: 2 -> 0; matrix products, arithmetic and copies ran while one was open for 0% -> 0% of each run, Pallas kernels for 0% -> 0%
where the time goes in v3:
time: 210 us
  Pallas kernels  181 us (86%)
  other arithmetic  14.9 us (7%)
  local copies, waits for them, and re-layouts  8.72 us (4%)
  matrix products  3.59 us (2%)
    pallas_call x1, Pallas kernels, on_device(): pl.pallas_call(pair_kernel, out_shape=(jax.ShapeDtypeStruct((row_blocks,...  132 us
    pallas_call x1, Pallas kernels, on_device(): pl.pallas_call(functools.partial(image_kernel, n_row, n_col), out_shape=(...  28.4 us
    pallas_call x1, Pallas kernels, on_device(): pl.pallas_call(functools.partial(gather_kernel, n_row, n_col), out_shape=...  20 us
    another operation x6, other arithmetic, symmetric_solve(): factor = jnp.linalg.cholesky(balanced)  7.2 us
    another operation x4, other arithmetic, symmetric_solve(): lax.linalg.triangular_solve(factor, middle, left_side=True, lower=True, t...  6.17 us

profile of v3, /device:TPU:0, one launch (start us, length us, event | category | flops | bytes accessed | tf_op | source)
XLA Modules:
  0.0 209.6 jit_solution(18139072583401109899)
XLA Ops:
  1.3 0.7 convert_element_type.13
  2.1 0.7 copy-done.8
  2.9 0.8 copy-done
  3.8 0.7 pad_maximum_fusion
  4.5 20.0 %gather.1 = (bf16[4,4,48,256]{3,2,1,0:T(8,128)(2,1)}, bf16[8,4,48,256]{3,2,1,0:T(8,128)(2,1)}) custom-call(bf16[4,48,256]{2,1,0:T(8,128)(2,1)} %get-tuple-element.23.row_in, bf16[4,48,256]{2,1,0:T(8,128)(2,1)} %get-tuple-element.22.col_in), custom_call_target="tpu_custom_call" | custom-call | tf_op jit(solution)/shard_map/gather/pallas_call | solution.py:298
  24.5 1.0 slice_bitcast_fusion
  25.5 1.7 slice.57.row_vec
  27.2 0.7 slice.56.far
  27.9 0.8 slice.58.col_vec
  28.8 1.3 copy.17.near
  30.1 132.3 %pairs.2 = (bf16[16,32,256]{2,1,0:T(8,128)(2,1)}, bf16[32,32,256]{2,1,0:T(8,128)(2,1)}, f32[4,32,256]{2,1,0:T(8,128)}) custom-call(s32[2,1536]{1,0:T(2,128)} %pairs.3, s32[1]{0:T(128)S(6)} %copy.27.count, bf16[16,256,16]{2,1,0:T(8,128)(2,1)} %copy.17.near, bf16[32,16,256]{2,1,0:T(8,128)(2,1)} %slice.56.far, bf16[16,32,256]{2,1,0:T(8,128)(2,1)} %slice.57.row_vec, ...), custom_call_target="tpu_custom_call" | custom-call | tf_op jit(solution)/shard_map/pairs/pallas_call | solution.py:315
  162.4 28.4 %image.1 = (f32[32,1024]{1,0:T(8,128)}, f32[64,128]{1,0:T(8,128)}) custom-call(bf16[16,32,256]{2,1,0:T(8,128)(2,1)} %get-tuple-element.15.row_part, bf16[32,32,256]{2,1,0:T(8,128)(2,1)} %get-tuple-element.16.col_part, f32[4,32,256]{2,1,0:T(8,128)} %get-tuple-element.17.own_product, f32[32,1024]{1,0:T(8,128)} %direction.1, f32[32,1024]{1,0:T(8,128)} %residual.1), custom_call_target="tpu_custom_call" | custom-call | tf_op jit(solution)/shard_map/image/pallas_call | solution.py:330
  190.9 0.9 slice.50
  191.9 2.9 %cholesky.55 = f32[32,32]{1,0:T(8,128)S(1)} custom-call(f32[32,32]{1,0:T(8,128)S(1)} %fusion.7), custom_call_target="Cholesky" | custom-call | tf_op jit(solution)/shard_map/jit(cholesky)/cholesky | solution.py:37
  194.9 0.6 compare_reduce_fusion
  195.5 0.7 fusion.2
  196.2 2.4 %custom-call.13 = f32[1,32,32]{1,2,0:T(8,128)S(1)} custom-call(f32[1,32,32]{2,1,0:T(8,128)S(1)} %fusion.2), custom_call_target="InvertDiagBlocksLowerTriangular" | custom-call | tf_op jit(solution)/shard_map/triangular_solve/custom-call.2 | solution.py:39
  198.9 2.9 %cholesky.44 = f32[32,32]{1,0:T(8,128)S(1)} custom-call(f32[32,32]{1,0:T(8,128)S(1)} %fusion.14), custom_call_target="Cholesky" | custom-call | tf_op jit(solution)/shard_map/jit(cholesky)/cholesky | solution.py:37
  201.9 0.6 compare_reduce_fusion.1
  202.5 0.7 fusion.1
  203.2 2.4 %custom-call.11 = f32[1,32,32]{1,2,0:T(8,128)S(1)} custom-call(f32[1,32,32]{2,1,0:T(8,128)S(1)} %fusion.1), custom_call_target="InvertDiagBlocksLowerTriangular" | custom-call | tf_op jit(solution)/shard_map/triangular_solve/custom-call.2 | solution.py:39
  206.1 0.3 convolution_subtract_fusion
  207.6 1.0 convolution_add_fusion
  208.6 1.0 convolution_add_fusion.1
  (52 shorter events, 2.4 us)
Async XLA Ops:
  2.1 0.7 copy-start.8
  2.8 0.9 copy-start
  24.5 2.7 %copy-start.2 = (bf16[8,4,48,256]{3,2,1,0:T(8,128)(2,1)S(1)}, bf16[8,4,48,256]{3,2,1,0:T(8,128)(2,1)}, u32[]{:S(2)}) copy-start(bf16[8,4,48,256]{3,2,1,0:T(8,128)(2,1)} %get-tuple-element.14) | copy-start | bytes 2359300
  190.8 0.9 copy-start.5
  198.8 7.2 %copy-start.3 = (f32[32,1024]{1,0:T(8,128)S(1)}, f32[32,1024]{1,0:T(8,128)}, u32[]{:S(2)}) copy-start(f32[32,1024]{1,0:T(8,128)} %residual.1) | copy-start | bytes 393220
  198.8 7.2 %copy-start.7 = (f32[32,1024]{1,0:T(8,128)S(1)}, f32[32,1024]{1,0:T(8,128)}, u32[]{:S(2)}) copy-start(f32[32,1024]{1,0:T(8,128)} %get-tuple-element.19) | copy-start | bytes 393220
  206.4 1.1 copy-start.4
  206.7 0.9 copy-start.1
  207.6 1.0 copy-start.6

commit v4 on v3

--- a/solution.py
+++ b/solution.py
@@ -1,4 +1,5 @@
 import functools
+import math
 
 import jax
 import jax.numpy as jnp
@@ -9,7 +10,7 @@
 
 TILE = 128
 FEATURES = 16
-UNROLL = 2
+UNROLL = 8
 BLOCK = 2 * TILE
 
 AMPLITUDE = 0.025
@@ -83,13 +84,17 @@
 
 
 def pair_kernel(
-    pairs, count, near, far, row_vec, col_vec, row_out, col_out, own_out, col_acc, floor
+    cells, count, near, row_pack, col_pack, row_out, col_out, own_out, col_acc, floor
 ):
-    row_blocks, col_blocks = near.shape[0], far.shape[0]
+    row_blocks, col_blocks = row_pack.shape[0], col_pack.shape[0]
+    probes = row_out.shape[1]
+    row_vec, col_vec = row_pack.at[:, :probes], col_pack.at[:, :probes]
+    far = col_pack.at[:, probes:]
     own_blocks = own_out.shape[0]
     stride = 2 * col_blocks
     scale = AMPLITUDE / 256.0
     live = count[0]
+    unroll = math.gcd(UNROLL, col_blocks)
     col_acc[...] = jnp.zeros_like(col_acc)
 
     @pl.loop(0, 2 * row_blocks * stride // 16)
@@ -98,7 +103,7 @@
             floor[step * 16 + k] = 16.0
 
     def mark(slot):
-        floor[pairs[0, slot] * stride + pairs[1, slot]] = 1e-20
+        floor[cells[slot]] = 1e-20
 
     whole = live // 8
 
@@ -122,14 +127,14 @@
     @pl.loop(0, row_blocks)
     def _(i):
         def several(step, total):
-            results = [products(i, step * UNROLL + k) for k in range(UNROLL)]
+            results = [products(i, step * unroll + k) for k in range(unroll)]
             for k, (forward, backward) in enumerate(results):
                 total = total + forward
-                col_acc[step * UNROLL + k] += backward
+                col_acc[step * unroll + k] += backward
             return total
 
-        start = jnp.zeros(row_vec.shape[1:], jnp.float32)
-        total = lax.fori_loop(0, col_blocks // UNROLL, several, start)
+        start = jnp.zeros(row_out.shape[1:], jnp.float32)
+        total = lax.fori_loop(0, col_blocks // unroll, several, start)
         row_out[i] = (scale * total).astype(row_out.dtype)
 
     row_base = lax.axis_index("col") * own_blocks
@@ -309,9 +314,9 @@
     )(row_in, col_in)
     row_pack = row_pack.reshape(-1, *row_in.shape[1:])
     col_pack = col_pack.reshape(-1, *col_in.shape[1:])
-    row_vec, near = row_pack[:, :probes], row_pack[:, probes:].transpose(0, 2, 1)
-    col_vec, far = col_pack[:, :probes], col_pack[:, probes:]
-    row_blocks, col_blocks = row_vec.shape[0], col_vec.shape[0]
+    near = row_pack[:, probes:].transpose(0, 2, 1)
+    row_blocks, col_blocks = row_pack.shape[0], col_pack.shape[0]
+    cells = tile_pairs[0] * (2 * col_blocks) + tile_pairs[1]
     row_part, col_part, own_product = pl.pallas_call(
         pair_kernel,
         out_shape=(
@@ -319,14 +324,14 @@
             jax.ShapeDtypeStruct((col_blocks, probes, BLOCK), jnp.bfloat16),
             jax.ShapeDtypeStruct((own_blocks, probes, BLOCK), jnp.float32),
         ),
-        in_specs=[smem, smem, vmem, vmem, vmem, vmem],
+        in_specs=[smem, smem, vmem, vmem, vmem],
         out_specs=(vmem, vmem, vmem),
         scratch_shapes=[
             pltpu.VMEM((col_blocks, probes, BLOCK), jnp.float32),
             pltpu.SMEM((4 * row_blocks * col_blocks,), jnp.float32),
         ],
         name="pairs",
-    )(tile_pairs, pair_count, near, far, row_vec, col_vec)
+    )(cells, pair_count, near, row_pack, col_pack)
     applied, gram = pl.pallas_call(
         functools.partial(image_kernel, n_row, n_col),
         out_shape=(

time: 210 us -> 196 us (0.933)
  Pallas kernels: 181 us -> 170 us
  local copies, waits for them, and re-layouts: 8.72 us -> 4.75 us
    pallas_call x1, Pallas kernels: 132 us -> 118 us  [on_device(): pl.pallas_call(pair_kernel, out_shape=(jax.ShapeDtypeStruct((row_blocks,...]
    pallas_call x1, Pallas kernels: 28.4 us -> 32.1 us  [on_device(): pl.pallas_call(functools.partial(image_kernel, n_row, n_col), out_shape=(...]
    slice x3 -> x0, local copies, waits for them, and re-layouts: 3.25 us -> none  [the longest x1 1.69 us: on_device(): row_pack[:, :probes]]
where the time goes in v4:
time: 196 us; the launch traced here: 195 us
  Pallas kernels  170 us (87%)
  other arithmetic  15.6 us (8%)
  local copies, waits for them, and re-layouts  4.75 us (2%)
  matrix products  3.59 us (2%)
    pallas_call x1, Pallas kernels, on_device(): pl.pallas_call(pair_kernel, out_shape=(jax.ShapeDtypeStruct((row_blocks,...  118 us
    pallas_call x1, Pallas kernels, on_device(): pl.pallas_call(functools.partial(image_kernel, n_row, n_col), out_shape=(...  32.1 us
    pallas_call x1, Pallas kernels, on_device(): pl.pallas_call(functools.partial(gather_kernel, n_row, n_col), out_shape=...  20 us
    another operation x6, other arithmetic, symmetric_solve(): factor = jnp.linalg.cholesky(balanced)  7.2 us
    another operation x4, other arithmetic, symmetric_solve(): lax.linalg.triangular_solve(factor, middle, left_side=True, lower=True, t...  6.17 us

profile of v4, /device:TPU:0, one launch (start us, length us, event | category | flops | bytes accessed | tf_op | source)
XLA Modules:
  0.0 195.3 jit_solution(7271408617441229180)
XLA Ops:
  1.3 1.4 add_reduce_fusion.cells
  3.0 0.8 copy-done
  3.8 0.7 pad_maximum_fusion
  4.5 20.0 %gather.1 = (bf16[4,4,48,256]{3,2,1,0:T(8,128)(2,1)}, bf16[8,4,48,256]{3,2,1,0:T(8,128)(2,1)}) custom-call(bf16[4,48,256]{2,1,0:T(8,128)(2,1)} %get-tuple-element.23.row_in, bf16[4,48,256]{2,1,0:T(8,128)(2,1)} %get-tuple-element.22.col_in), custom_call_target="tpu_custom_call" | custom-call | tf_op jit(solution)/shard_map/gather/pallas_call | solution.py:303
  24.5 0.9 slice_bitcast_fusion
  25.5 1.3 copy.17.near
  26.8 117.7 %pairs.1 = (bf16[16,32,256]{2,1,0:T(8,128)(2,1)}, bf16[32,32,256]{2,1,0:T(8,128)(2,1)}, f32[4,32,256]{2,1,0:T(8,128)}) custom-call(s32[1536]{0:T(1024)} %add_reduce_fusion.cells, s32[1]{0:T(128)S(6)} %copy.27.count, bf16[16,256,16]{2,1,0:T(8,128)(2,1)} %copy.17.near, bf16[16,48,256]{2,1,0:T(8,128)(2,1)} %bitcast.74, bf16[32,48,256]{2,1,0:T(8,128)(2,1)} %bitcast.72), custom_call_target="tpu_custom_call" | custom-call | tf_op jit(solution)/shard_map/pairs/pallas_call | solution.py:320
  144.5 32.1 %image.1 = (f32[32,1024]{1,0:T(8,128)}, f32[64,128]{1,0:T(8,128)}) custom-call(bf16[16,32,256]{2,1,0:T(8,128)(2,1)} %get-tuple-element.15.row_part, bf16[32,32,256]{2,1,0:T(8,128)(2,1)} %get-tuple-element.16.col_part, f32[4,32,256]{2,1,0:T(8,128)} %get-tuple-element.17.own_product, f32[32,1024]{1,0:T(8,128)} %direction.1, f32[32,1024]{1,0:T(8,128)} %residual.1), custom_call_target="tpu_custom_call" | custom-call | tf_op jit(solution)/shard_map/image/pallas_call | solution.py:335
  176.6 0.9 slice.46
  177.7 2.9 %cholesky.55 = f32[32,32]{1,0:T(8,128)S(1)} custom-call(f32[32,32]{1,0:T(8,128)S(1)} %fusion.7), custom_call_target="Cholesky" | custom-call | tf_op jit(solution)/shard_map/jit(cholesky)/cholesky | solution.py:38
  180.7 0.6 compare_reduce_fusion
  181.3 0.7 fusion.2
  182.0 2.4 %custom-call.13 = f32[1,32,32]{1,2,0:T(8,128)S(1)} custom-call(f32[1,32,32]{2,1,0:T(8,128)S(1)} %fusion.2), custom_call_target="InvertDiagBlocksLowerTriangular" | custom-call | tf_op jit(solution)/shard_map/triangular_solve/custom-call.2 | solution.py:40
  184.7 2.9 %cholesky.44 = f32[32,32]{1,0:T(8,128)S(1)} custom-call(f32[32,32]{1,0:T(8,128)S(1)} %fusion.14), custom_call_target="Cholesky" | custom-call | tf_op jit(solution)/shard_map/jit(cholesky)/cholesky | solution.py:38
  187.7 0.6 compare_reduce_fusion.1
  188.3 0.7 fusion.1
  189.0 2.4 %custom-call.11 = f32[1,32,32]{1,2,0:T(8,128)S(1)} custom-call(f32[1,32,32]{2,1,0:T(8,128)S(1)} %fusion.1), custom_call_target="InvertDiagBlocksLowerTriangular" | custom-call | tf_op jit(solution)/shard_map/triangular_solve/custom-call.2 | solution.py:40
  191.4 0.3 fusion.9
  191.8 0.3 convolution_subtract_fusion
  192.2 0.2 fusion.17
  192.6 0.2 convolution_add_fusion.2
  192.9 0.2 fusion.3
  193.4 1.0 convolution_add_fusion
  194.4 1.0 convolution_add_fusion.1
  (48 shorter events, 1.5 us)
Async XLA Ops:
  1.3 1.4 copy-start.7
  2.9 0.9 copy-start
  176.6 0.9 copy-start.4
  184.6 7.2 %copy-start.2 = (f32[32,1024]{1,0:T(8,128)S(1)}, f32[32,1024]{1,0:T(8,128)}, u32[]{:S(2)}) copy-start(f32[32,1024]{1,0:T(8,128)} %residual.1) | copy-start | bytes 393220
  184.6 7.2 %copy-start.6 = (f32[32,1024]{1,0:T(8,128)S(1)}, f32[32,1024]{1,0:T(8,128)}, u32[]{:S(2)}) copy-start(f32[32,1024]{1,0:T(8,128)} %get-tuple-element.19) | copy-start | bytes 393220
  192.2 1.1 copy-start.3
  192.5 0.9 copy-start.1
  193.4 1.0 copy-start.5
